TPU v7x, 256 devices: a whole 4x4x8 slice. The times are simulated.
256 devices in a mesh: store: 8 (over y, core), tensor: 32 (over z, x).
Axes of the slice: x: 4, y: 4, z: 8, core: 2. Of those that a mesh axis runs over, the one named last changes fastest.
Arguments:
- decoder_rows: bfloat16 [16384, 4096], P(('store', 'tensor')), may hold values from -45 to 45
- q_weight: bfloat16 [4096, 4096], P(None, 'tensor'), may hold values from -0.09375 to 0.09375
- kv_weight: bfloat16 [2, 896, 4096], P(None, None, 'tensor'), may hold values from -0.1875 to 0.1875
- out_weight: bfloat16 [4096, 4096], P('tensor'), may hold values from -0.5 to 0.5
- store_tiles: bfloat16 [4096, 128, 896], P('store', 'tensor'), may hold values from -6 to 6
- neighbour_shard: int32 [256, 2], replicated, may hold values from 0 to 7, all different within a row; in each aligned block of 32 rows (0 to 31, 32 to 63, ...) at most 12 rows name the same one
- neighbour_tile: int32 [256, 2], replicated, may hold values from 0 to 511
Outputs:
- cross: bfloat16 [16384, 4096], P(('store', 'tensor'))
Inputs may be any that keep to these rules, and one draw needn't show every extreme that they name: `neighbour_shard`: each block's 2 neighbours lie in different shards; among the 32 blocks of one sequence no shard is named more than 12 times, and in some sequence one shard is named exactly 12 times.
All inputs are finite; a program needn't handle non-finite values.
Results may differ from a plain program's by a relative error of at most 0.023.
Values may be sent and summed in bfloat16 or wider, within the bound.
No kernel may reach another device: no remote copies, remote signals or barrier semaphores. Data moves between devices by JAX's collectives and lax.ppermute only.
A program may use at most 128 MiB of HBM per device.

v0:
```python
import math
import jax
import jax.numpy as jnp
from jax import lax
from jax.sharding import PartitionSpec as P

HD = 128
BLOCK = 64
NTOK = 128
NEIGH = 2


def body(
    decoder_rows, q_weight, kv_weight, out_weight, store_tiles, neighbour_shard, neighbour_tile
):
    tensor_count = lax.axis_size("tensor")
    store_count = lax.axis_size("store")
    my_sequence = lax.axis_index("store")
    local_rows = decoder_rows.shape[0]
    seq_len = local_rows * tensor_count
    block_count = seq_len // BLOCK
    request_count = block_count * NEIGH
    capacity = 3 * request_count // (2 * store_count)
    head_cols = q_weight.shape[1]
    head_count = head_cols // HD
    q_factor = 1.0 / math.sqrt(HD)
    rows_wide = decoder_rows.astype(jnp.float32)
    normed = (
        rows_wide * lax.rsqrt(jnp.mean(rows_wide * rows_wide, axis=1, keepdims=True) + 1e-05)
    ).astype(jnp.bfloat16)
    queries = (
        jnp.dot(
            lax.all_gather(normed, "tensor", axis=0, tiled=True),
            q_weight,
            preferred_element_type=jnp.float32,
        )
        * q_factor
    ).astype(jnp.bfloat16)
    shard_table = neighbour_shard.reshape(store_count, request_count)
    tile_table = neighbour_tile.reshape(store_count, request_count)
    positions = jnp.arange(request_count, dtype=jnp.int32)
    before_mask = positions[None, :] < positions[:, None]
    same_shard = shard_table[:, :, None] == shard_table[:, None, :]
    rank_table = jnp.sum((same_shard & before_mask[None]).astype(jnp.int32), axis=2)
    served_here = shard_table == my_sequence
    slot_ids = jnp.arange(capacity, dtype=jnp.int32)
    slot_match = (
        served_here[:, :, None] & (rank_table[:, :, None] == slot_ids[None, None, :])
    ).astype(jnp.int32)
    slot_tile = jnp.sum(slot_match * tile_table[:, :, None], axis=1)
    outgoing = jnp.take(store_tiles, slot_tile.reshape(-1), axis=0)
    arrived = lax.all_to_all(outgoing, "store", split_axis=0, concat_axis=0, tiled=True)
    own_shard = lax.dynamic_index_in_dim(shard_table, my_sequence, 0, keepdims=False)
    own_rank = lax.dynamic_index_in_dim(rank_table, my_sequence, 0, keepdims=False)
    slot_index = own_shard * capacity + own_rank
    projected = jnp.einsum(
        "rne,ced->rncd",
        jnp.take(lax.all_gather(arrived, "tensor", axis=1, tiled=True), slot_index, axis=0),
        kv_weight,
        preferred_element_type=jnp.float32,
    )
    keys_values = projected.astype(jnp.bfloat16)
    keyed = keys_values.reshape(block_count, NEIGH * NTOK, 2, head_count, HD)
    query_blocks = queries.reshape(block_count, BLOCK, head_count, HD)
    scores = jnp.einsum(
        "cqhd,ckhd->chqk", query_blocks, keyed[:, :, 0], preferred_element_type=jnp.float32
    )
    expo_scores = jnp.exp(scores)
    weights = (expo_scores / jnp.sum(expo_scores, axis=3, keepdims=True)).astype(jnp.bfloat16)
    attended = jnp.einsum(
        "chqk,ckhd->cqhd", weights, keyed[:, :, 1], preferred_element_type=jnp.float32
    )
    attended = attended.astype(jnp.bfloat16).reshape(seq_len, head_cols)
    return lax.psum_scatter(
        jnp.dot(attended, out_weight, preferred_element_type=jnp.float32).astype(jnp.bfloat16),
        "tensor",
        scatter_dimension=0,
        tiled=True,
    )


def solution(mesh):
    in_specs = (
        P(("store", "tensor"), None),
        P(None, "tensor"),
        P(None, None, "tensor"),
        P("tensor", None),
        P("store", "tensor", None),
        P(),
        P(),
    )
    out_specs = P(("store", "tensor"), None)
    return jax.shard_map(body, mesh=mesh, in_specs=in_specs, out_specs=out_specs, check_vma=False)
```

profile of v0, /device:TPU:16, one launch (start us, length us, event | category | flops | bytes accessed | tf_op | source)
XLA Modules:
  0.0 625.0 jit_solution(14406171586889492786)
XLA Ops:
  6.5 1.4 fusion.12
  8.0 2.0 fusion.13
  9.9 0.0 all-gather.5.cloned.1.call-update
  10.0 0.0 all-gather.3.cloned.1.call-start
  10.0 0.8 copy.26
  10.8 0.1 reshape.146
  11.0 0.8 copy.27
  11.8 0.1 mul.46
  11.9 0.3 convert_reduce_fusion
  12.3 0.3 select_reduce_fusion
  12.5 0.1 copy.28
  12.6 0.1 reshape.148
  12.7 0.1 reshape.147
  12.8 3.2 gather_fusion
  16.1 0.4 broadcast_select_fusion
  16.5 14.0 %all_to_all.5 = bf16[96,4,896]{2,1,0:T(4,128)(2,1)S(1)} all-to-all(bf16[96,4,896]{2,1,0:T(4,128)(2,1)S(1)} %broadcast_select_fusion), channel_id=1, replica_groups=mesh['store'=8,'tensor'=32] {'store'}, dimensions={0} | all-to-all | bytes 1376256 | tf_op jit(solution)/shard_map/all_to_all | solution.py:52
  30.4 0.9 copy.30
  31.4 0.0 all-gather.3.cloned.1.call-update
  31.4 0.2 reduce-scatter.2.cloned.1.call-start
  31.7 121.8 %all-gather.5.cloned.1.call-done = bf16[2048,4096]{1,0:T(8,128)(2,1)} async-done(((bf16[64,4096]{1,0:T(8,128)(2,1)}), bf16[2048,4096]{1,0:T(8,128)(2,1)}) %all-gather.5.cloned.1.call-update) | async-done | bytes 16777232 | tf_op jit(solution)/shard_map/all_gather | solution.py:33
  153.5 8.2 %fusion.8 = bf16[2048,128]{1,0:T(8,128)(2,1)S(1)} fusion(bf16[2048,4096]{1,0:T(8,128)(2,1)} %all-gather.5.cloned.1.call-done, bf16[4096,128]{1,0:T(8,128)(2,1)S(1)} %copy-done.1), kind=kOutput, calls=%fused_computation.10 | convolution fusion | flops 2148007936 | bytes 18350080 | tf_op jit(solution)/shard_map/dot_general | solution.py:32
  161.7 158.3 %all-gather.3.cloned.1.call-done = bf16[96,128,896]{2,0,1:T(8,128)(2,1)} async-done(((bf16[96,4,896]{2,0,1:T(8,128)(2,1)}), bf16[96,128,896]{2,0,1:T(8,128)(2,1)}) %all-gather.3.cloned.1.call-update) | async-done | bytes 22020112 | tf_op jit(solution)/shard_map/all_gather | solution.py:58
  320.0 21.1 %copy.31 = bf16[96,128,896]{2,1,0:T(8,128)(2,1)} copy(bf16[96,128,896]{2,0,1:T(8,128)(2,1)} %all-gather.3.cloned.1.call-done) | data formatting | bytes 44040192 | tf_op jit(solution)/shard_map/all_gather | solution.py:58
  341.1 15.7 %gather_fusion.1 = bf16[64,128,896]{2,1,0:T(8,128)(2,1)} fusion(bf16[96,128,896]{2,1,0:T(8,128)(2,1)} %copy.31, s32[1024]{0:T(1024)S(1)} %pad_clamp_fusion), kind=kCustom, calls=%fused_computation.1 | custom fusion | bytes 29360384 | tf_op jit(solution)/shard_map/jit(_take)/gather | solution.py:58
  356.8 0.0 copy-done.2
  356.8 9.8 %fusion.5 = bf16[64,128,2,128]{3,1,2,0:T(8,128)(2,1)S(1)} fusion(bf16[64,128,896]{2,1,0:T(8,128)(2,1)} %gather_fusion.1, pred[64]{0:T(512)(128)(4,1)S(1)} %get-tuple-element.5, bf16[2,896,128]{2,1,0:T(8,128)(2,1)S(1)} %copy-done.2), kind=kOutput, calls=%fused_computation.8 | convolution fusion | flops 3767533568 | bytes 19333184 | tf_op jit(solution)/shard_map/rne,ced->rncd/dot_general | solution.py:56
  366.6 0.3 copy.32
  366.9 0.9 exponential_reduce_fusion
  367.8 0.6 fusion.11
  368.5 8.3 %convolution_convert_fusion = bf16[2048,4096]{1,0:T(8,128)(2,1)} fusion(bf16[2048,128]{1,0:T(8,128)(2,1)S(1)} %bitcast.45, bf16[128,4096]{1,0:T(8,128)(2,1)S(1)} %copy-done), kind=kOutput, calls=%fused_computation.2 | convolution fusion | flops 2155872256 | bytes 18350080 | tf_op jit(solution)/shard_map/dot_general | solution.py:75
  376.7 0.0 reduce-scatter.2.cloned.1.call-update
  376.8 241.7 %reduce-scatter.2.cloned.1.call-done = bf16[64,4096]{1,0:T(8,128)(2,1)} async-done(((bf16[2048,4096]{1,0:T(8,128)(2,1)}), bf16[64,4096]{1,0:T(8,128)(2,1)}) %reduce-scatter.2.cloned.1.call-update) | async-done | bytes 524304 | tf_op jit(solution)/shard_map/reduce_scatter | solution.py:74
  (15 shorter events, 0.1 us)
Async XLA Ops:
  6.5 361.9 %copy-start = (bf16[128,4096]{1,0:T(8,128)(2,1)S(1)}, bf16[128,4096]{1,0:T(8,128)(2,1)}, u32[]{:S(2)}) copy-start(bf16[128,4096]{1,0:T(8,128)(2,1)} %param.10) | copy-start | bytes 3145732
  6.5 146.9 %copy-start.1 = (bf16[4096,128]{1,0:T(8,128)(2,1)S(1)}, bf16[4096,128]{1,0:T(8,128)(2,1)}, u32[]{:S(2)}) copy-start(bf16[4096,128]{1,0:T(8,128)(2,1)} %param.8) | copy-start | bytes 3145732
  6.5 146.9 %all-gather.5.cloned.1.call-start = ((), (), s32[]{:S(2)}) async-start(), calls=%async_computation.3 | async-start | bytes 17301504 | tf_op jit(solution)/shard_map/all_gather | solution.py:33
  10.0 310.0 %all-gather.3.cloned.1.call-start = ((), (), s32[]{:S(2)}) async-start(), calls=%async_computation.2 | async-start | bytes 22708224 | tf_op jit(solution)/shard_map/all_gather | solution.py:58
  31.4 587.1 %reduce-scatter.2.cloned.1.call-start = ((), (), s32[]{:S(2)}) async-start(), calls=%async_computation.4 | async-start | bytes 17301504 | tf_op jit(solution)/shard_map/reduce_scatter | solution.py:74
  341.1 15.7 %copy-start.2 = (bf16[2,896,128]{2,1,0:T(8,128)(2,1)S(1)}, bf16[2,896,128]{2,1,0:T(8,128)(2,1)}, u32[]{:S(2)}) copy-start(bf16[2,896,128]{2,1,0:T(8,128)(2,1)} %param.9) | copy-start | bytes 1376260
Sparse Core Ops, SparseCore 0:
  10.1 143.3 all-gather.4
  156.0 163.8 all-gather.2
  376.9 241.5 reduce-scatter.1
where the time goes:
time: 625 us
  waiting for transfers between devices  522 us (84%)
  local copies, waits for them, and re-layouts  43.4 us (7%)
  matrix products  27.8 us (4%)
  blocking collectives  14 us (2%)
  between operations  13.3 us (2%)
    reduce_scatter x1, waiting for transfers between devices, body(): lax.psum_scatter(jnp.dot(attended, out_weight, preferred_element_type=jnp...  242 us
    all_gather x1, waiting for transfers between devices, body(): lax.all_gather(arrived, 'tensor', axis=1, tiled=True)  158 us
    all_gather x1, waiting for transfers between devices, body(): lax.all_gather(normed, 'tensor', axis=0, tiled=True)  122 us
    all_gather x1, local copies, waits for them, and re-layouts, body(): lax.all_gather(arrived, 'tensor', axis=1, tiled=True)  21.1 us
    gather x1, local copies, waits for them, and re-layouts, body(): jnp.take(lax.all_gather(arrived, 'tensor', axis=1, tiled=True), slot_inde...  15.7 us
    all_to_all x1, blocking collectives, body(): lax.all_to_all(outgoing, 'store', split_axis=0, concat_axis=0, tiled=True)  14 us
  transfers between devices with their start and end apart: 3, of which 3 were waited for; matrix products, arithmetic and copies ran while one was open for 2% of the time, Pallas kernels for 0%

commit v1 on v0

--- a/solution.py
+++ b/solution.py
@@ -8,6 +8,18 @@
 BLOCK = 64
 NTOK = 128
 NEIGH = 2
+
+
+def make_face_for(vector):
+    return jnp.concatenate(
+        lax.all_to_all(
+            jnp.stack(tuple((vector for _ in range(lax.axis_size("tensor"))))),
+            axis_name="tensor",
+            split_axis=0,
+            concat_axis=0,
+        ),
+        1,
+    )
 
 
 def body(
@@ -55,7 +67,7 @@
     slot_index = own_shard * capacity + own_rank
     projected = jnp.einsum(
         "rne,ced->rncd",
-        jnp.take(lax.all_gather(arrived, "tensor", axis=1, tiled=True), slot_index, axis=0),
+        jnp.take(make_face_for(arrived), slot_index, axis=0),
         kv_weight,
         preferred_element_type=jnp.float32,
     )

time: 625 us -> 971 us (1.55)
  waiting for transfers between devices: 522 us -> 850 us
  starting transfers between devices: 0.27 us -> 11.8 us
    all_gather x1, waiting for transfers between devices: 122 us -> 407 us  [body(): lax.all_gather(normed, 'tensor', axis=0, tiled=True)]
    all_to_all x0 -> x1, waiting for transfers between devices: none -> 180 us  [make_face_for(): lax.all_to_all(jnp.stack(tuple((vector for _ in range(lax.axis_size('tens...]
    all_gather x1 -> x0, waiting for transfers between devices: 158 us -> none  [body(): lax.all_gather(arrived, 'tensor', axis=1, tiled=True)]
    reduce_scatter x1, waiting for transfers between devices: 242 us -> 263 us  [body(): lax.psum_scatter(jnp.dot(attended, out_weight, preferred_element_type=jnp...]
    reshape x0 -> x1, local copies, waits for them, and re-layouts: none -> 21.1 us  [make_face_for(): jnp.concatenate(lax.all_to_all(jnp.stack(tuple((vector for _ in range(lax...]
    all_gather x1 -> x0, local copies, waits for them, and re-layouts: 21.1 us -> none  [body(): lax.all_gather(arrived, 'tensor', axis=1, tiled=True)]
    all_to_all x0 -> x1, starting transfers between devices: none -> 11.6 us  [make_face_for(): lax.all_to_all(jnp.stack(tuple((vector for _ in range(lax.axis_size('tens...]
  transfers between devices with their start and end apart: 3 -> 3, of which waited for: 3 -> 3; matrix products, arithmetic and copies ran while one was open for 2% -> 1% of each run, Pallas kernels for 0% -> 0%
where the time goes in v1:
time: 971 us
  waiting for transfers between devices  850 us (88%)
  local copies, waits for them, and re-layouts  51.5 us (5%)
  matrix products  27.8 us (3%)
  blocking collectives  14 us (1%)
  between operations  13.6 us (1%)
  starting transfers between devices  11.8 us (1%)
    all_gather x1, waiting for transfers between devices, body(): lax.all_gather(normed, 'tensor', axis=0, tiled=True)  407 us
    reduce_scatter x1, waiting for transfers between devices, body(): lax.psum_scatter(jnp.dot(attended, out_weight, preferred_element_type=jnp...  263 us
    all_to_all x1, waiting for transfers between devices, make_face_for(): lax.all_to_all(jnp.stack(tuple((vector for _ in range(lax.axis_size('tens...  180 us
    reshape x1, local copies, waits for them, and re-layouts, make_face_for(): jnp.concatenate(lax.all_to_all(jnp.stack(tuple((vector for _ in range(lax...  21.1 us
  transfers between devices with their start and end apart: 3, of which 3 were waited for; matrix products, arithmetic and copies ran while one was open for 1% of the time, Pallas kernels for 0%

profile of v1, /device:TPU:16, one launch (start us, length us, event | category | flops | bytes accessed | tf_op | source)
XLA Modules:
  0.0 970.5 jit_solution(7705670971197079789)
XLA Ops:
  6.6 0.9 copy.22
  7.5 0.1 reshape.154
  7.6 0.3 convert_reduce_fusion
  7.9 0.8 copy.23
  8.7 0.1 mul.46
  8.9 0.3 select_reduce_fusion
  9.1 0.1 copy.24
  9.2 0.1 reshape.156
  9.3 0.1 reshape.155
  9.4 3.2 gather_fusion
  12.7 0.4 broadcast_select_fusion
  13.1 14.0 %all_to_all.10 = bf16[96,4,896]{2,1,0:T(4,128)(2,1)S(1)} all-to-all(bf16[96,4,896]{2,1,0:T(4,128)(2,1)S(1)} %broadcast_select_fusion), channel_id=1, replica_groups=mesh['store'=8,'tensor'=32] {'store'}, dimensions={0} | all-to-all | bytes 1376256 | tf_op jit(solution)/shard_map/all_to_all | solution.py:64
  27.0 0.1 copy.26
  27.1 8.8 stack.2
  35.9 11.6 %all-to-all-start.1 = ((bf16[32,96,4,896]{3,1,2,0:T(8,128)(2,1)}), bf16[32,96,4,896]{3,1,2,0:T(8,128)(2,1)}, u32[]{:S(2)}, u32[]{:S(2)}) async-start(bf16[32,96,4,896]{3,1,2,0:T(8,128)(2,1)} %stack.2), calls=%async_computation.1 | async-start | bytes 44040192 | tf_op jit(solution)/shard_map/all_to_all | solution.py:15
  47.5 0.0 all-gather.2.cloned.1.call-start
  47.6 0.2 fusion.12
  47.8 1.0 fusion.13
  48.7 0.0 all-gather.2.cloned.1.call-update
  48.8 0.2 reduce-scatter.2.cloned.1.call-start
  49.1 406.5 %all-gather.2.cloned.1.call-done = bf16[2048,4096]{1,0:T(8,128)(2,1)} async-done(((bf16[64,4096]{1,0:T(8,128)(2,1)}), bf16[2048,4096]{1,0:T(8,128)(2,1)}) %all-gather.2.cloned.1.call-update) | async-done | bytes 16777232 | tf_op jit(solution)/shard_map/all_gather | solution.py:45
  455.6 8.2 fusion.8
  463.8 180.1 %all-to-all-done.1 = bf16[32,96,4,896]{3,1,2,0:T(8,128)(2,1)} async-done(((bf16[32,96,4,896]{3,1,2,0:T(8,128)(2,1)}), bf16[32,96,4,896]{3,1,2,0:T(8,128)(2,1)}, u32[]{:S(2)}, u32[]{:S(2)}) %all-to-all-start.1) | async-done | bytes 22020128 | tf_op jit(solution)/shard_map/all_to_all | solution.py:15
  643.9 21.1 %copy.27 = bf16[96,128,896]{2,1,0:T(8,128)(2,1)} copy(bf16[96,128,896]{2,0,1:T(8,128)(2,1)} %bitcast.3) | data formatting | bytes 44040192 | tf_op jit(solution)/shard_map/reshape | solution.py:14
  665.1 15.7 %gather_fusion.1 = bf16[64,128,896]{2,1,0:T(8,128)(2,1)} fusion(bf16[96,128,896]{2,1,0:T(8,128)(2,1)} %copy.27, s32[1024]{0:T(1024)S(1)} %pad_clamp_fusion), kind=kCustom, calls=%fused_computation.1 | custom fusion | bytes 29360384 | tf_op jit(solution)/shard_map/jit(_take)/gather | solution.py:70
  680.8 9.8 %fusion.5 = bf16[64,128,2,128]{3,1,2,0:T(8,128)(2,1)S(1)} fusion(bf16[64,128,896]{2,1,0:T(8,128)(2,1)} %gather_fusion.1, pred[64]{0:T(512)(128)(4,1)S(1)} %get-tuple-element.5, bf16[2,896,128]{2,1,0:T(8,128)(2,1)S(1)} %copy-done.3), kind=kOutput, calls=%fused_computation.8 | convolution fusion | flops 3767533568 | bytes 19333184 | tf_op jit(solution)/shard_map/rne,ced->rncd/dot_general | solution.py:68
  690.5 0.3 copy.28
  690.8 0.9 exponential_reduce_fusion
  691.8 0.6 fusion.11
  692.4 8.3 convolution_convert_fusion
  700.7 0.0 reduce-scatter.2.cloned.1.call-update
  700.7 262.9 %reduce-scatter.2.cloned.1.call-done = bf16[64,4096]{1,0:T(8,128)(2,1)} async-done(((bf16[2048,4096]{1,0:T(8,128)(2,1)}), bf16[64,4096]{1,0:T(8,128)(2,1)}) %reduce-scatter.2.cloned.1.call-update) | async-done | bytes 524304 | tf_op jit(solution)/shard_map/reduce_scatter | solution.py:86
  (17 shorter events, 0.1 us)
Async XLA Ops:
  6.5 685.9 %copy-start = (bf16[128,4096]{1,0:T(8,128)(2,1)S(1)}, bf16[128,4096]{1,0:T(8,128)(2,1)}, u32[]{:S(2)}) copy-start(bf16[128,4096]{1,0:T(8,128)(2,1)} %param.10) | copy-start | bytes 3145732
  35.9 11.6 %copy-start.1 = (bf16[64,4096]{1,0:T(8,128)(2,1)S(1)}, bf16[64,4096]{1,0:T(8,128)(2,1)}, u32[]{:S(2)}) copy-start(bf16[64,4096]{1,0:T(8,128)(2,1)} %param.7) | copy-start | bytes 1572868
  35.9 419.7 %copy-start.2 = (bf16[4096,128]{1,0:T(8,128)(2,1)S(1)}, bf16[4096,128]{1,0:T(8,128)(2,1)}, u32[]{:S(2)}) copy-start(bf16[4096,128]{1,0:T(8,128)(2,1)} %param.8) | copy-start | bytes 3145732
  35.9 608.0 %all-to-all-start.1 = ((bf16[32,96,4,896]{3,1,2,0:T(8,128)(2,1)}), bf16[32,96,4,896]{3,1,2,0:T(8,128)(2,1)}, u32[]{:S(2)}, u32[]{:S(2)}) async-start(bf16[32,96,4,896]{3,1,2,0:T(8,128)(2,1)} %stack.2), calls=%async_computation.1 | async-start | bytes 44040192 | tf_op jit(solution)/shard_map/all_to_all | solution.py:15
  47.5 408.1 %all-gather.2.cloned.1.call-start = ((), (), s32[]{:S(2)}) async-start(), calls=%async_computation.3 | async-start | bytes 17301504 | tf_op jit(solution)/shard_map/all_gather | solution.py:45
  48.8 914.9 %reduce-scatter.2.cloned.1.call-start = ((), (), s32[]{:S(2)}) async-start(), calls=%async_computation.4 | async-start | bytes 17301504 | tf_op jit(solution)/shard_map/reduce_scatter | solution.py:86
  665.1 15.7 %copy-start.3 = (bf16[2,896,128]{2,1,0:T(8,128)(2,1)S(1)}, bf16[2,896,128]{2,1,0:T(8,128)(2,1)}, u32[]{:S(2)}) copy-start(bf16[2,896,128]{2,1,0:T(8,128)(2,1)} %param.9) | copy-start | bytes 1376260
Sparse Core Ops, SparseCore 0:
  50.9 404.6 all-gather.1
  700.8 262.7 reduce-scatter.1
